TPU v7x, 256 devices: a whole 4x4x8 slice. The times are simulated.
256 devices in a mesh: gx: 32 (over x, y, core), gy: 8 (over z).
Axes of the slice: x: 4, y: 4, z: 8, core: 2. Of those that a mesh axis runs over, the one named last changes fastest.
Arguments:
- hidden: bfloat16 [1024, 16384], P('gx', 'gy'), may hold values from -40 to 40
- lm_head: bfloat16 [16384, 65536], P('gy', 'gx'), may hold values from -1 to 1
- parent: int32 [1024], replicated, may hold values from 0 to 1023, as said below
- draft_token: int32 [1024], replicated, may hold values from 0 to 65535
- draft_prob: float32 [1024], replicated, may hold values from 0.01 to 1
- uniforms: float32 [1024], replicated, may hold values from 0.01 to 1
- node_count: int32 [16], replicated, may hold values from 1 to 64, as said below
- accepted_end: int32 [16], replicated, may hold values from 0 to 63, as said below
Outputs:
- vertex_accept_slack: float32 [1024], P('gx')
- lineage_least_slack: float32 [1024], P('gx')
- extra_draw_score: float32 [16, 65536], P(None, 'gx')
Inputs may be any that keep to these rules, and one draw needn't show every extreme that they name: A node's parent lies in the same sequence at a lower slot; slot 0 of each sequence is its own parent. `node_count`: some sequence has all 64 slots live. `accepted_end`: the slot of a live node of that sequence.
All inputs are finite; a program needn't handle non-finite values.
Results may differ from a plain program's by a relative error of at most 0.0003.
Values may be sent and summed in bfloat16 or wider, within the bound.
A program may use at most 64 MiB of HBM per device.

v0:
```python
import jax
import jax.numpy as jnp
from jax import lax
from jax.sharding import Mesh
from jax.sharding import PartitionSpec as P

GX = ("gx_0", "gx_1", "gx_2")


big_margin = 10000.0


def in_order(tiles, dim):
    shape = list(tiles.shape[1:])
    shape[dim] *= tiles.shape[0]
    return jnp.moveaxis(tiles, 0, dim).reshape(shape)


def all_blocks(x, axes, sequence):
    tiles = x[None]
    for k in sequence:
        tiles = lax.all_gather(tiles, axes[k], axis=0, tiled=True)
    held = [lax.axis_size(axes[k]) for k in reversed(sequence)]
    tiles = tiles.reshape(*held, *x.shape)
    turned = sorted(range(len(sequence)), key=lambda place: sequence[len(sequence) - 1 - place])
    return tiles.transpose(*turned, *range(len(sequence), tiles.ndim)).reshape(-1, *x.shape)


def whole_of(x, axes, sequence, dim):
    return in_order(all_blocks(x, axes, sequence), dim)


def from_everyone(x, axis):
    copies = jnp.broadcast_to(x, (lax.axis_size(axis), *x.shape))
    return lax.all_to_all(copies, axis, split_axis=0, concat_axis=0, tiled=True)


def all_in_one(x, axis):
    leaves = jax.tree.leaves(x)
    sequence = sorted(range(len(leaves)), key=lambda k: -leaves[k].size)
    width = (1, *leaves[sequence[0]].shape)[-1]
    lines = [
        jnp.pad(leaves[k].reshape(-1), (0, -leaves[k].size % width)).reshape(-1, width)
        for k in sequence
    ]
    both, at, found = (from_everyone(jnp.concatenate(lines), axis), 0, {})
    for k, line in zip(sequence, lines):
        section = both[:, at : at + len(line)].reshape(len(both), -1)
        found[k] = section[:, : leaves[k].size].reshape(-1, *leaves[k].shape)
        at += len(line)
    numbers = iter(range(len(leaves)))
    return jax.tree.map(lambda _: found[next(numbers)], x)


def joined_by_halves(pieces, combine):
    while len(jax.tree.leaves(pieces)[0]) > 1:
        pieces = jax.vmap(combine)(
            *(jax.tree.map(lambda part: part[side::2], pieces) for side in (0, 1))
        )
    return jax.tree.map(lambda part: part[0], pieces)


def combined_all(x, axis, combine):
    pieces = all_in_one(x, axis)
    return joined_by_halves(pieces, combine)


def taken_together(x, axis):
    return from_everyone(x, axis).sum(axis=0)


def together(arrays, axis):
    ends = [0]
    for a in arrays:
        ends.append(ends[-1] + a.size)
    subtotal = taken_together(jnp.concatenate([a.ravel() for a in arrays]), axis)
    return tuple((subtotal[b:e].reshape(a.shape) for a, b, e in zip(arrays, ends, ends[1:])))


def combine_stats(first, second):
    top = jnp.maximum(first[0], second[0])
    total = first[1] * jnp.exp(first[0] - top) + second[1] * jnp.exp(second[0] - top)
    return (top, total, first[2] + second[2])


def local(hidden, lm_head, parent, draft_token, draft_prob, uniforms, node_count, accepted_end):
    out_rows = hidden.shape[0]
    out_start = lax.axis_index(GX) * out_rows
    node_total = parent.shape[0]
    seq_total = node_count.shape[0]
    tree_size = node_total // seq_total
    width = lm_head.shape[1]
    vocab_base = lax.axis_index(GX) * width
    leaf_entries = jnp.arange(seq_total, dtype=jnp.int32) * tree_size + accepted_end
    columns = whole_of(hidden, GX, (1, 0, 2), 0)
    row_count = node_total // lax.axis_size("gy")
    start_row = lax.axis_index("gy") * row_count
    emitted_scores = lax.psum_scatter(
        jnp.dot(columns, lm_head, preferred_element_type=jnp.float32),
        "gy",
        scatter_dimension=0,
        tiled=True,
    )
    own_parent = parent - start_row
    own_token = draft_token - vocab_base
    hit_mask = (own_parent >= 0) & (own_parent < row_count) & (own_token >= 0) & (own_token < width)
    picked = emitted_scores[
        jnp.clip(own_parent, 0, row_count - 1), jnp.clip(own_token, 0, width - 1)
    ]
    target_part = jnp.where(hit_mask, picked, 0.0)
    local_max = jnp.max(emitted_scores, axis=1)
    local_sum = jnp.sum(jnp.exp(emitted_scores - local_max[:, None]), axis=1)
    row_max, row_sum, target_part = combined_all(
        (local_max, local_sum, target_part), GX, combine_stats
    )
    row_log_total = row_max + jnp.log(row_sum)
    total_part = lax.dynamic_update_slice_in_dim(
        jnp.zeros((node_total,), jnp.float32), row_log_total, start_row, 0
    )
    own_end = leaf_entries - start_row
    owned = (own_end >= 0) & (own_end < row_count)
    end_part = jnp.where(owned[:, None], emitted_scores[jnp.clip(own_end, 0, row_count - 1)], 0.0)
    partition_function, target, leaf_scores = together((total_part, target_part, end_part), "gy")
    extra_draw_score = leaf_scores - partition_function[leaf_entries][:, None]
    margin = target - partition_function[parent] - jnp.log(draft_prob) - jnp.log(uniforms)
    node_index = jnp.arange(node_total, dtype=jnp.int32)
    local_index = node_index % tree_size
    live_mask = local_index < node_count[node_index // tree_size]
    root_mask = parent == node_index
    spare_mask = jnp.logical_or(root_mask, jnp.logical_not(live_mask))
    all_margin = jnp.where(spare_mask, 0.0, margin)
    path_min = jnp.where(root_mask, big_margin, margin)
    ancestor = parent
    for _ in range((tree_size - 1).bit_length()):
        path_min = jnp.minimum(path_min, path_min[ancestor])
        ancestor = ancestor[ancestor]
    all_path = jnp.where(spare_mask, 0.0, path_min)
    vertex_accept_slack = lax.dynamic_slice_in_dim(all_margin, out_start, out_rows, 0)
    lineage_least_slack = lax.dynamic_slice_in_dim(all_path, out_start, out_rows, 0)
    return (vertex_accept_slack, lineage_least_slack, extra_draw_score)


def solution(mesh):
    finer = Mesh(mesh.devices.reshape(4, 4, 2, mesh.shape["gy"]), ("gx_0", "gx_1", "gx_2", "gy"))
    placed = (P(GX, "gy"), P("gy", GX), P(), P(), P(), P(), P(), P())
    return jax.shard_map(
        local, mesh=finer, in_specs=placed, out_specs=(P(GX), P(GX), P(None, GX)), check_vma=False
    )
```

profile of v0, /device:TPU:1, one launch (start us, length us, event | category | flops | bytes accessed | tf_op | source)
XLA Modules:
  0.0 307.7 jit_solution(15902408323733157968)
XLA Ops:
  7.2 0.0 all-gather.4.cloned.1.call-start
  7.2 13.3 %all-gather = bf16[128,2048]{1,0:T(8,128)(2,1)} all-gather(bf16[32,2048]{1,0:T(8,128)(2,1)} %param.8), channel_id=2, replica_groups=mesh['gx_0'=4,'gx_1'=4,'gx_2'=2,'gy'=8] {'gx_1'}, dimensions={0}, use_global_device_ids=true | all-gather | bytes 655360 | tf_op jit(solution)/shard_map/all_gather | solution.py:22
  20.5 0.0 all-gather.4.cloned.1.call-update
  20.5 0.0 all-gather.6.cloned.1.call-start
  20.6 37.3 %all-gather.4.cloned.1.call-done = bf16[16,32,2048]{2,1,0:T(8,128)(2,1)} async-done(((bf16[4,32,2048]{2,1,0:T(8,128)(2,1)}), bf16[16,32,2048]{2,1,0:T(8,128)(2,1)}) %all-gather.4.cloned.1.call-update) | async-done | bytes 2097168 | tf_op jit(solution)/shard_map/all_gather | solution.py:22
  57.9 0.0 all-gather.6.cloned.1.call-update
  57.9 0.0 reduce-scatter.2.cloned.1.call-start
  57.9 21.7 %all-gather.6.cloned.1.call-done = bf16[32,32,2048]{2,1,0:T(8,128)(2,1)} async-done(((bf16[16,32,2048]{2,1,0:T(8,128)(2,1)}), bf16[32,32,2048]{2,1,0:T(8,128)(2,1)}) %all-gather.6.cloned.1.call-update) | async-done | bytes 4194320 | tf_op jit(solution)/shard_map/all_gather | solution.py:22
  79.6 2.7 copy.16
  82.3 2.0 copy-done.8
  84.3 11.0 %fusion.17 = f32[1024,2048]{1,0:T(8,128)} fusion(bf16[1024,2048]{1,0:T(8,128)(2,1)S(1)} %bitcast.55, bf16[2048,2048]{1,0:T(8,128)(2,1)S(1)} %copy-done.8), kind=kOutput, calls=%fused_computation.94 | convolution fusion | flops 8589934592 | bytes 20971520 | tf_op jit(solution)/shard_map/dot_general | solution.py:99
  95.3 0.0 reduce-scatter.2.cloned.1.call-update
  95.3 0.6 copy-done
  96.0 4.5 %gather_fusion.4 = s32[1024]{0:T(1024)S(1)} fusion(s32[1024]{0:T(1024)S(1)} %copy-done, s32[1024]{0:T(1024)S(1)} %get-tuple-element.19), kind=kCustom, calls=%fused_computation.4 | custom fusion | bytes 12288 | tf_op jit(solution)/shard_map/gather | solution.py:136
  100.6 90.3 %reduce-scatter.2.cloned.1.call-done = f32[128,2048]{1,0:T(8,128)} async-done(((f32[1024,2048]{1,0:T(8,128)}), f32[128,2048]{1,0:T(8,128)}) %reduce-scatter.2.cloned.1.call-update) | async-done | bytes 1048592 | tf_op jit(solution)/shard_map/reduce_scatter | solution.py:98
  190.9 1.4 reduce_max.9
  192.3 1.5 exponential_reduce_fusion
  193.9 8.6 %gather_fusion = f32[1024]{0:T(1024)S(1)} fusion(f32[128,2048]{1,0:T(8,128)S(1)} %copy-done.1, s32[1024]{0:T(1024)S(1)} %get-tuple-element.20), kind=kCustom, calls=%fused_computation | custom fusion | bytes 16384 | tf_op jit(solution)/shard_map/gather | solution.py:107
  202.5 0.9 broadcast_in_dim.66
  203.4 7.6 %all-to-all-start = ((f32[32,3,1024]{2,1,0:T(4,128)}), f32[32,3,1024]{2,1,0:T(4,128)S(1)}, u32[]{:S(2)}, u32[]{:S(2)}) async-start(f32[32,3,1024]{2,1,0:T(4,128)} %broadcast_in_dim.66), calls=%async_computation.1 | async-start | bytes 1048576 | tf_op jit(solution)/shard_map/all_to_all | solution.py:35
  211.0 4.5 %gather_fusion.6 = s32[1024]{0:T(1024)S(1)} fusion(s32[1024]{0:T(1024)S(1)} %gather_fusion.4, s32[1024]{0:T(1024)S(1)} %broadcast_clamp_fusion.4), kind=kCustom, calls=%fused_computation.6 | custom fusion | bytes 12288 | tf_op jit(solution)/shard_map/gather | solution.py:136
  215.6 0.6 gather_fusion.1
  216.2 0.1 select_bitcast_fusion
  216.3 6.3 %all-to-all-done = f32[32,3,1024]{2,1,0:T(4,128)S(1)} async-done(((f32[32,3,1024]{2,1,0:T(4,128)}), f32[32,3,1024]{2,1,0:T(4,128)S(1)}, u32[]{:S(2)}, u32[]{:S(2)}) %all-to-all-start) | async-done | bytes 393248 | tf_op jit(solution)/shard_map/all_to_all | solution.py:35
  222.6 0.3 fusion.15
  222.9 0.1 copy_bitcast_fusion
  223.6 0.1 bitcast_dynamic-update-slice_fusion
  223.8 1.6 broadcast_in_dim.70
  225.4 4.1 %all-to-all-start.1 = ((f32[8,1,34816]{2,1,0:T(1,128)}), f32[8,1,34816]{2,1,0:T(1,128)S(1)}, u32[]{:S(2)}, u32[]{:S(2)}) async-start(f32[8,1,34816]{2,1,0:T(1,128)} %broadcast_in_dim.70), calls=%async_computation.2 | async-start | bytes 2228224 | tf_op jit(solution)/shard_map/all_to_all | solution.py:35
  229.5 4.5 %gather_fusion.8 = s32[1024]{0:T(1024)S(1)} fusion(s32[1024]{0:T(1024)S(1)} %gather_fusion.6, s32[1024]{0:T(1024)S(1)} %broadcast_clamp_fusion.3), kind=kCustom, calls=%fused_computation.8 | custom fusion | bytes 12288 | tf_op jit(solution)/shard_map/gather | solution.py:136
  234.0 4.5 %gather_fusion.10 = s32[1024]{0:T(1024)S(1)} fusion(s32[1024]{0:T(1024)S(1)} %gather_fusion.8, s32[1024]{0:T(1024)S(1)} %broadcast_clamp_fusion.2), kind=kCustom, calls=%fused_computation.10 | custom fusion | bytes 12288 | tf_op jit(solution)/shard_map/gather | solution.py:136
  238.6 4.5 %gather_fusion.12 = s32[1024]{0:T(1024)S(1)} fusion(s32[1024]{0:T(1024)S(1)} %gather_fusion.10, s32[1024]{0:T(1024)S(1)} %broadcast_clamp_fusion.1), kind=kCustom, calls=%fused_computation.12 | custom fusion | bytes 12288 | tf_op jit(solution)/shard_map/gather | solution.py:136
  243.5 0.7 fusion.16
  244.2 4.4 %compare_select_fusion.6 = s32[1024,1]{0,1:T(1,128)S(1)} fusion(s32[]{:T(128)} %bitcast.9, s32[]{:T(128)} %bitcast.10, s32[]{:T(128)} %bitcast.11, s32[]{:T(128)} %bitcast.12, s32[]{:T(128)} %bitcast.13, s32[]{:T(128)} %bitcast.15, s32[]{:T(128)} %bitcast.14), kind=kLoop, calls=%fused_computation.38 | loop fusion | flops 23552 | bytes 4124 | tf_op jit(solution)/shard_map/gather | solution.py:128
  248.6 11.5 %all-to-all-done.1 = f32[8,1,34816]{2,1,0:T(1,128)S(1)} async-done(((f32[8,1,34816]{2,1,0:T(1,128)}), f32[8,1,34816]{2,1,0:T(1,128)S(1)}, u32[]{:S(2)}, u32[]{:S(2)}) %all-to-all-start.1) | async-done | bytes 1114144 | tf_op jit(solution)/shard_map/all_to_all | solution.py:35
  260.1 0.8 reduce_sum.19
  261.0 4.5 %gather_fusion.2 = f32[1024]{0:T(1024)S(1)} fusion(f32[1024]{0:T(1024)S(1)} %slice.224, s32[1024]{0:T(1024)S(1)} %get-tuple-element.19), kind=kCustom, calls=%fused_computation.2 | custom fusion | bytes 12288 | tf_op jit(solution)/shard_map/gather | solution.py:125
  265.5 4.5 %gather_fusion.3 = f32[1024]{0:T(1024)S(1)} fusion(f32[1024]{0:T(1024)S(1)} %get-tuple-element.5, s32[1024]{0:T(1024)S(1)} %get-tuple-element.19), kind=kCustom, calls=%fused_computation.3 | custom fusion | bytes 12288 | tf_op jit(solution)/shard_map/gather | solution.py:135
  270.1 4.5 %gather_fusion.5 = f32[1024]{0:T(1024)S(1)} fusion(f32[1024]{0:T(1024)S(1)} %min.46, s32[1024]{0:T(1024)S(1)} %broadcast_clamp_fusion.4), kind=kCustom, calls=%fused_computation.5 | custom fusion | bytes 12288 | tf_op jit(solution)/shard_map/gather | solution.py:135
  274.7 4.5 %gather_fusion.7 = f32[1024]{0:T(1024)S(1)} fusion(f32[1024]{0:T(1024)S(1)} %min.47, s32[1024]{0:T(1024)S(1)} %broadcast_clamp_fusion.3), kind=kCustom, calls=%fused_computation.7 | custom fusion | bytes 12288 | tf_op jit(solution)/shard_map/gather | solution.py:135
  279.2 4.5 %gather_fusion.9 = f32[1024]{0:T(1024)S(1)} fusion(f32[1024]{0:T(1024)S(1)} %min.48, s32[1024]{0:T(1024)S(1)} %broadcast_clamp_fusion.2), kind=kCustom, calls=%fused_computation.9 | custom fusion | bytes 12288 | tf_op jit(solution)/shard_map/gather | solution.py:135
  283.8 4.5 %gather_fusion.11 = f32[1024]{0:T(1024)S(1)} fusion(f32[1024]{0:T(1024)S(1)} %min.49, s32[1024]{0:T(1024)S(1)} %broadcast_clamp_fusion.1), kind=kCustom, calls=%fused_computation.11 | custom fusion | bytes 12288 | tf_op jit(solution)/shard_map/gather | solution.py:135
  288.3 4.5 %gather_fusion.13 = f32[1024]{0:T(1024)S(1)} fusion(f32[1024]{0:T(1024)S(1)} %min.50, s32[1024]{0:T(1024)S(1)} %broadcast_clamp_fusion), kind=kCustom, calls=%fused_computation.13 | custom fusion | bytes 12288 | tf_op jit(solution)/shard_map/gather | solution.py:135
  292.8 5.7 %minimum_select_fusion = (f32[1024]{0:T(1024)S(1)}, pred[1024]{0:T(1024)(128)(4,1)S(1)}) fusion(f32[1024]{0:T(1024)S(1)} %min.50, f32[1024]{0:T(1024)S(1)} %gather_fusion.13, pred[1024]{0:T(1024)(128)(4,1)S(1)} %get-tuple-element.7, pred[1024]{0:T(1024)(128)(4,1)S(1)} %compare_reduce_fusion, pred[1024]{0:T(1024)(128)(4,1)S(1)} %compare_reduce_fusion.1, ...), kind=kLoop, calls=%fused_computation.66 | loop fusion | flops 20480 | bytes 27684 | tf_op jit(solution)/shard_map/jit(_where)/select_n | solution.py:137
  298.6 0.6 dynamic_slice.6
  299.1 0.6 dynamic_slice.7
  299.8 0.6 gather_fusion.14
  300.4 0.7 broadcast_subtract_fusion
  (94 shorter events, 1.2 us)
Async XLA Ops:
  7.2 50.7 %all-gather.4.cloned.1.call-start = ((), (), s32[]{:S(2)}) async-start(), calls=%async_computation.3 | async-start | bytes 2621440 | tf_op jit(solution)/shard_map/all_gather | solution.py:22
  20.5 59.1 %all-gather.6.cloned.1.call-start = ((), (), s32[]{:S(2)}) async-start(), calls=%async_computation.4 | async-start | bytes 6291456 | tf_op jit(solution)/shard_map/all_gather | solution.py:22
  57.9 133.0 %reduce-scatter.2.cloned.1.call-start = ((), (), s32[]{:S(2)}) async-start(), calls=%async_computation.5 | async-start | bytes 9437184 | tf_op jit(solution)/shard_map/reduce_scatter | solution.py:98
  79.6 4.6 %copy-start.8 = (bf16[2048,2048]{1,0:T(8,128)(2,1)S(1)}, bf16[2048,2048]{1,0:T(8,128)(2,1)}, u32[]{:S(2)}) copy-start(bf16[2048,2048]{1,0:T(8,128)(2,1)} %param.9) | copy-start | bytes 25165828
  95.3 0.7 copy-start
  95.3 0.7 copy-start.4
  95.3 5.2 %copy-start.7 = (s32[16]{0:T(128)S(1)}, s32[16]{0:T(128)}, u32[]{:S(2)}) copy-start(s32[16]{0:T(128)} %param.15) | copy-start | bytes 196
  190.9 3.0 copy-start.1
  203.4 19.2 %all-to-all-start = ((f32[32,3,1024]{2,1,0:T(4,128)}), f32[32,3,1024]{2,1,0:T(4,128)S(1)}, u32[]{:S(2)}, u32[]{:S(2)}) async-start(f32[32,3,1024]{2,1,0:T(4,128)} %broadcast_in_dim.66), calls=%async_computation.1 | async-start | bytes 1048576 | tf_op jit(solution)/shard_map/all_to_all | solution.py:35
  225.4 34.8 %all-to-all-start.1 = ((f32[8,1,34816]{2,1,0:T(1,128)}), f32[8,1,34816]{2,1,0:T(1,128)S(1)}, u32[]{:S(2)}, u32[]{:S(2)}) async-start(f32[8,1,34816]{2,1,0:T(1,128)} %broadcast_in_dim.70), calls=%async_computation.2 | async-start | bytes 2228224 | tf_op jit(solution)/shard_map/all_to_all | solution.py:35
  234.0 9.5 %copy-start.3 = (s32[16]{0:T(128)S(1)}, s32[16]{0:T(128)}, u32[]{:S(2)}) copy-start(s32[16]{0:T(128)} %param.14) | copy-start | bytes 196
  238.6 26.9 %copy-start.5 = (f32[1024]{0:T(1024)S(1)}, f32[1024]{0:T(1024)}, u32[]{:S(2)}) copy-start(f32[1024]{0:T(1024)} %param.13) | copy-start | bytes 12292
  238.6 26.9 %copy-start.6 = (f32[1024]{0:T(1024)S(1)}, f32[1024]{0:T(1024)}, u32[]{:S(2)}) copy-start(f32[1024]{0:T(1024)} %param.12) | copy-start | bytes 12292
  260.9 9.1 %copy-start.2 = (f32[34816]{0:T(1024)}, f32[34816]{0:T(1024)S(1)}, u32[]{:S(2)}) copy-start(f32[34816]{0:T(1024)S(1)} %reduce_sum.19) | copy-start | bytes 417796
  283.7 16.0 %slice-start = ((f32[34816]{0:T(1024)}), f32[32768]{0:T(1024)S(1)}, s32[]{:S(2)}) async-start(f32[34816]{0:T(1024)} %copy-done.2), calls=%async_computation.6 | async-start | bytes 262144 | tf_op jit(solution)/shard_map/slice | solution.py:77
Sparse Core Ops, SparseCore 0:
  20.6 37.1 all-gather.3
  59.7 19.9 all-gather.5
  95.4 95.4 reduce-scatter.1
where the time goes:
time: 308 us
  waiting for transfers between devices  167 us (54%)
  local copies, waits for them, and re-layouts  74.7 us (24%)
  other arithmetic  15.4 us (5%)
  between operations  14.3 us (5%)
  blocking collectives  13.3 us (4%)
  starting transfers between devices  11.8 us (4%)
  matrix products  11 us (4%)
    reduce_scatter x1, waiting for transfers between devices, local(): lax.psum_scatter(jnp.dot(columns, lm_head, preferred_element_type=jnp.flo...  90.3 us
    all_gather x2, waiting for transfers between devices, all_blocks(): tiles = lax.all_gather(tiles, axes[k], axis=0, tiled=True)  59 us
    gather x6, local copies, waits for them, and re-layouts, local(): path_min = jnp.minimum(path_min, path_min[ancestor])  27.2 us
    gather x5, local copies, waits for them, and re-layouts, local(): ancestor = ancestor[ancestor]  22.6 us
    all_to_all x2, waiting for transfers between devices, from_everyone(): return lax.all_to_all(copies, axis, split_axis=0, concat_axis=0, tiled=True)  17.8 us
    all_gather x1, blocking collectives, all_blocks(): tiles = lax.all_gather(tiles, axes[k], axis=0, tiled=True)  13.3 us
    all_to_all x2, starting transfers between devices, from_everyone(): return lax.all_to_all(copies, axis, split_axis=0, concat_axis=0, tiled=True)  11.7 us
    dot_general x1, matrix products, local(): jnp.dot(columns, lm_head, preferred_element_type=jnp.float32)  11 us
  transfers between devices with their start and end apart: 5, of which 5 were waited for; matrix products, arithmetic and copies ran while one was open for 9% of the time, Pallas kernels for 0%

commit v1 on v0

v1 whole, which is shorter than its diff:
```python
import functools

import jax
import jax.numpy as jnp
from jax import lax
from jax.experimental import pallas as pl
from jax.experimental.pallas import tpu as pltpu
from jax.sharding import Mesh
from jax.sharding import PartitionSpec as P

GX = ("gx_0", "gx_1", "gx_2")
ALL = ("gx_0", "gx_1", "gx_2", "gy")
NX, NY, NC, NZ = 4, 4, 2, 8
PLANE = NX * NY * NC
HALF = 16
TILE = 256
LONG = 4
BLOCKS = (48, 64, 128)
BIG = 10000.0
F32 = jnp.float32
BF16 = jnp.bfloat16
AT = pl.DeviceIdType.MESH


def iota(shape, dim):
    return lax.broadcasted_iota(jnp.int32, shape, dim)


def to_column(row, rows):
    spread = jnp.broadcast_to(row, (rows, row.shape[1]))
    keep = iota(spread.shape, 0) == iota(spread.shape, 1)
    return jnp.sum(jnp.where(keep, spread, 0.0), axis=1, keepdims=True)


def to_row(column, lanes):
    spread = jnp.broadcast_to(column, (column.shape[0], lanes))
    keep = iota(spread.shape, 0) == iota(spread.shape, 1)
    return jnp.sum(jnp.where(keep, spread, 0.0), axis=0, keepdims=True)


def two_rows(first, second):
    lines = iota((16, first.shape[1]), 0)
    return jnp.where(lines == 0, first, jnp.where(lines == 1, second, 0.0)).astype(BF16)


def plan(parent, counts, ends, token, prob, uniform, vec, which):
    shape = parent.shape
    lines, lanes = iota((1, 128), 0), iota((1, 128), 1)
    total = jnp.zeros((1, 128), F32)
    before = (iota((128, 128), 0) < iota((128, 128), 1)).astype(F32).astype(BF16)
    order, reads = [], []
    for t in range(shape[0]):
        second = lanes >= 64
        slot = jnp.where(second, lanes - 64, lanes)
        live = slot < jnp.where(second, counts[2 * t + 1], counts[2 * t])
        end = slot == jnp.where(second, ends[2 * t + 1], ends[2 * t])
        up = parent[t : t + 1, :] - t * 128
        root = up == lanes
        child = jnp.where(live & jnp.logical_not(root), up.astype(F32), -1.0)
        column = to_column(child, 128)
        hit = (column == iota((128, 128), 1).astype(F32)).astype(F32)
        needed = jnp.max(hit, axis=0, keepdims=True)
        plain = jnp.where(end, 0.0, needed)
        vec[0 + t : 1 + t, :] = up.astype(F32)
        vec[16 + t : 17 + t, :] = plain
        vec[24 + t : 25 + t, :] = jnp.where(end, jnp.where(second, 2 * t + 1, 2 * t), -1).astype(F32)
        vec[32 + t : 33 + t, :] = jnp.where(root, 1.0, jnp.where(live, 0.0, 1.0))
        vec[40 + t : 41 + t, :] = root.astype(F32)
        within = jnp.dot(
            jnp.broadcast_to(plain, (16, 128)).astype(BF16), before, preferred_element_type=F32
        )[0:1, :]
        vec[56 + t : 57 + t, :] = within + total
        total = total + jnp.sum(plain, axis=1, keepdims=True)
    vec[8:16, :] = token[...].astype(F32)
    vec[48:56, :] = jnp.log(prob[...]) + jnp.log(uniform[...])
    size = jnp.max(total).astype(jnp.int32)
    which[0] = sum(jnp.where(size > NZ * (cap - 2), 1, 0) for cap in BLOCKS[:-1])


def kernel(
    cap, vec, own, head, out_v, out_l, out_e,
    w, hid, comp, acc, pick, tok, pp, reach, rq, rs, sq, ss,
    scores, tpk, send_a, recv_a, send_b, recv_b, ext,
    loc, gs, gr, pr, qs, qr, ps, pq, a_s, a_r, b_s, b_r, e_s, e_r,
):
    rows = cap * NZ
    nodes = tok.shape[1]
    groups = nodes // 128
    width = head.shape[1]
    part = hid.shape[2]
    tiles = width // TILE
    x, y = lax.axis_index("gx_0"), lax.axis_index("gx_1")
    c, z = lax.axis_index("gx_2"), lax.axis_index("gy")
    gx = (x * NY + y) * NC + c
    first = c == 0

    load_w = pltpu.make_async_copy(head, w, loc.at[2])
    load_w.start()
    own_rows = pl.ds(pl.multiple_of(gx * 2 * HALF, 2 * HALF), 2 * HALF)
    loads = [
        pltpu.make_async_copy(own.at[:, pl.ds(k * part, part)], hid.at[k, own_rows], loc.at[k])
        for k in range(2)
    ]
    for load in loads:
        load.start()

    xs = [lax.rem(x + d, NX) for d in range(NX)]
    ys = [lax.rem(y + d, NY) for d in range(NY)]
    peers = []
    for dx in (2, 1, 3, 0):
        for dy in (2, 1, 3, 0):
            for other in (1, 0):
                if dx or dy or other:
                    core = 1 - c if other else c
                    peers.append(((xs[dx] * NY + ys[dy]) * NC + core, (xs[dx], ys[dy], core, z)))
    stack = [(p, (x, y, c, p)) for p in (lax.rem(z + d, NZ) for d in (4, 3, 5, 2, 6, 1, 7))]

    barrier = pltpu.get_barrier_semaphore()
    for _, to in peers + stack:
        pl.semaphore_signal(barrier, inc=1, device_id=to, device_id_type=AT)
    for load in loads:
        load.wait()
    pl.semaphore_wait(barrier, len(peers) + len(stack))

    places = {}

    def block(da, db, h, core):
        straight = core == 0
        bx = lax.rem(x + jnp.where(straight, da, db), NX)
        by = lax.rem(y + jnp.where(straight, db, da), NY)
        at = (((bx * NY + by) * NC + core) * 2 + h) * HALF
        return pl.ds(pl.multiple_of(at, HALF), HALF)

    for da in range(4):
        for db in range(4):
            for h in range(2):
                places[da, db, h] = block(da, db, h, c)

    sent = []
    counts = {}

    def chip(axis, step):
        along_x = first if axis == 0 else jnp.logical_not(first)
        tx = lax.rem(x + jnp.where(along_x, step, 0) + NX, NX)
        ty = lax.rem(y + jnp.where(along_x, 0, step) + NY, NY)
        return (tx, ty, c, z)

    chips = {(axis, step): chip(axis, step) for axis in range(2) for step in (1, -1)}
    partner = (x, y, 1 - c, z)

    def push(k, da, db, h, arrival, to):
        here = hid.at[k, places[da, db, h]]
        n = counts.get((k, h), 0)
        counts[k, h] = n + 1
        copy = pltpu.make_async_remote_copy(
            src_ref=here, dst_ref=here, send_sem=gs.at[k, h, n], recv_sem=arrival,
            device_id=to, device_id_type=AT,
        )
        copy.start()
        sent.append(copy)

    def send(k, da, db, h, axis, step):
        ra = (da - step) % 4 if axis == 0 else da
        rb = (db - step) % 4 if axis == 1 else db
        push(k, da, db, h, gr.at[k, h, ra, rb], chips[axis, step])

    def share(k, da, db, h):
        push(k, da, db, h, pr.at[k, h, da, db], partner)

    def landed(ref, arrival):
        pltpu.make_async_remote_copy(
            src_ref=ref, dst_ref=ref, send_sem=gs.at[0, 0, 0], recv_sem=arrival,
            device_id=partner, device_id_type=AT,
        ).wait_recv()

    def arrive(k, da, db, h):
        landed(hid.at[k, places[da, db, h]], gr.at[k, h, da, db])

    def arrive_partner(k):
        for h in range(2):
            for da in range(4):
                for db in range(4):
                    landed(hid.at[k, block(da, db, h, 1 - c)], pr.at[k, h, da, db])

    sign = (1, -1)

    def level_0(k):
        for h in range(2):
            for axis in range(2):
                for step in (1, -1):
                    send(k, 0, 0, h, axis, step)
        for h in range(2):
            share(k, 0, 0, h)

    def level_1(k):
        for h in range(2):
            s = sign[h]
            for da, db in ((-s % 4, 0), (s % 4, 0), (0, -s % 4), (0, s % 4)):
                arrive(k, da, db, h)
                if db == 0:
                    if da == -s % 4:
                        send(k, da, db, h, 0, s)
                    send(k, da, db, h, 1, 1)
                    send(k, da, db, h, 1, -1)
                elif db == -s % 4:
                    send(k, da, db, h, 1, s)
                share(k, da, db, h)

    def level_2(k):
        for h in range(2):
            s = sign[h]
            arrive(k, 2, 0, h)
            send(k, 2, 0, h, 1, 1)
            send(k, 2, 0, h, 1, -1)
            share(k, 2, 0, h)
            for db in (-s % 4, s % 4):
                for da in (3, 1):
                    arrive(k, da, db, h)
                    if db == -s % 4:
                        send(k, da, db, h, 1, s)
                    share(k, da, db, h)
            arrive(k, 0, 2, h)
            share(k, 0, 2, h)

    def level_3(k):
        for h in range(2):
            s = sign[h]
            for db in (-s % 4, s % 4):
                arrive(k, 2, db, h)
                if db == -s % 4:
                    send(k, 2, db, h, 1, s)
                share(k, 2, db, h)
            for da in (3, 1):
                arrive(k, da, 2, h)
                share(k, da, 2, h)

    def level_4(k):
        for h in range(2):
            arrive(k, 2, 2, h)
            share(k, 2, 2, h)

    level_0(0)
    level_0(1)

    per = cap - 2
    order = vec[56:64, :]
    home = jnp.zeros_like(order)
    for i in range(1, NZ):
        home = home + (order >= float(i * per)).astype(F32)
    spot = home * cap + (order - home * per) + 2.0
    ends = vec[24:32, :]
    pair = jnp.floor(ends * 0.5)
    end_spot = jnp.where(ends >= 0.0, pair * cap + (ends - 2.0 * pair), -1.0)
    pos = jnp.where(vec[16:24, :] > 0.0, spot, end_spot)
    pos_id = pos.astype(jnp.int32)

    def mark(j, _):
        at = pl.ds(pl.multiple_of(j * 128, 128), 128)
        for t in range(groups):
            same = iota((128, 128), 0) + j * 128 == pos_id[t : t + 1, :]
            pick[at, t * 128 : (t + 1) * 128] = same.astype(F32).astype(BF16)
        return 0

    lax.fori_loop(0, rows // 128, mark, 0)
    level_1(0)
    level_1(1)

    token = vec[8:16, :].astype(jnp.int32) - gx * width

    def token_rows(j, _):
        at = pl.ds(pl.multiple_of(j * 128, 128), 128)
        for t in range(groups):
            same = iota((128, 128), 0) + j * 128 == token[t : t + 1, :]
            tok[at, t * 128 : (t + 1) * 128] = same.astype(F32).astype(BF16)
        return 0

    lax.fori_loop(0, width // 128, token_rows, 0)
    level_2(0)
    level_2(1)
    upper = jnp.floor(pos * (1.0 / 32.0))
    lower = pos - 32.0 * upper
    parents = vec[0:8, :].astype(jnp.int32)
    for t in range(groups):
        hit = (iota((128, 128), 0) == parents[t : t + 1, :]).astype(F32).astype(BF16)
        both = two_rows(upper[t : t + 1, :], lower[t : t + 1, :])
        got = jnp.dot(both, hit, preferred_element_type=F32)
        pp[t : t + 1, :] = got[0:1, :] * 32.0 + got[1:2, :]
    group = gx // 4
    up = vec[pl.ds(group, 1), :].astype(jnp.int32)
    line, lane_ids = iota((128, 128), 0), iota((128, 128), 1)
    reach[...] = jnp.where(line == up, 1.0, jnp.where(line == lane_ids, 1.0, 0.0))

    level_3(0)
    level_3(1)

    def spread(_, carry):
        now = reach[...].astype(BF16)
        reach[...] = jnp.minimum(jnp.dot(now, now, preferred_element_type=F32), 1.0)
        return carry

    lax.fori_loop(0, 6, spread, 0)
    level_4(0)

    def select(k):
        def body(j, _):
            lane = pl.ds(pl.multiple_of(j * TILE, TILE), TILE)
            comp[k, :, lane] = jnp.dot(
                pick[...], hid[k, :, lane], preferred_element_type=F32
            ).astype(BF16)
            return 0

        lax.fori_loop(0, part // TILE, body, 0)

    arrive_partner(0)
    select(0)
    level_4(1)
    load_w.wait()

    def lanes_of(j):
        return pl.ds(pl.multiple_of(j * TILE, TILE), TILE)

    def quantize(v, m, j):
        top = jnp.maximum(jnp.max(jnp.abs(v), axis=0, keepdims=True), 1e-30)
        ss[m, j] = top * (1.0 / 32767.0)
        sq[m, j] = jnp.round(v * (32767.0 / top)).astype(jnp.int32).astype(jnp.int16)

    above, below = (x, y, c, lax.rem(z + 1, NZ)), (x, y, c, lax.rem(z + NZ - 1, NZ))

    def ring_copies(m, j, way):
        to = above if (way == 0) == (m < LONG) else below
        return (
            pltpu.make_async_remote_copy(
                src_ref=sq.at[m, j], dst_ref=rq.at[m, j], send_sem=qs.at[m, j],
                recv_sem=qr.at[m, j], device_id=to, device_id_type=AT),
            pltpu.make_async_remote_copy(
                src_ref=ss.at[m, j], dst_ref=rs.at[m, j], send_sem=ps.at[m, j],
                recv_sem=pq.at[m, j], device_id=to, device_id_type=AT),
        )

    def rows_of(steps):
        d = lax.rem(z + steps + NZ, NZ)
        return pl.ds(pl.multiple_of(d * cap, 16), cap)

    def goal(m, way):
        s = 1 if way == 0 else -1
        return s * (LONG - m) if m < LONG else -s * (NZ - 1 - m)

    def forward(v, m, j, way):
        quantize(v, m, j)
        for copy in ring_copies(m, j, way):
            copy.start()

    def arrived(m, j, way):
        for copy in ring_copies(m, j, way):
            copy.wait_recv()
        return rq[m, j].astype(jnp.int32).astype(F32) * rs[m, j]

    def lower_half(j, _):
        acc[:, lanes_of(j)] = jnp.dot(comp[0], w[0:part, lanes_of(j)], preferred_element_type=F32)
        return 0

    lax.fori_loop(0, tiles, lower_half, 0)
    arrive_partner(1)
    select(1)

    def upper_half(jj, _):
        for way in range(2):
            j = jj * 2 + way
            acc[:, lanes_of(j)] += jnp.dot(
                comp[1], w[part : 2 * part, lanes_of(j)], preferred_element_type=F32
            )
            for m in (0, LONG):
                forward(acc[rows_of(goal(m, way)), lanes_of(j)], m, j, way)
        return 0

    lax.fori_loop(0, tiles // 2, upper_half, 0)

    for hop in range(1, LONG):
        def pass_on(jj, _, hop=hop):
            for way in range(2):
                j = jj * 2 + way
                for m in (hop, LONG + hop):
                    if m < NZ - 1:
                        got = arrived(m - 1, j, way)
                        forward(got + acc[rows_of(goal(m, way)), lanes_of(j)], m, j, way)
            return 0

        lax.fori_loop(0, tiles // 2, pass_on, 0)

    tpk[...] = jnp.zeros_like(tpk)

    def finish(jj, _):
        for way in range(2):
            j = jj * 2 + way
            v = acc[rows_of(0), lanes_of(j)] + arrived(NZ - 2, j, way) + arrived(LONG - 1, j, way)
            scores[:, lanes_of(j)] = v
            high = v.astype(BF16)
            rest = v - high.astype(F32)
            middle = rest.astype(BF16)
            low = (rest - middle.astype(F32)).astype(BF16)
            got = jnp.dot(
                jnp.concatenate([high, middle, low], axis=0), tok[lanes_of(j), :],
                preferred_element_type=F32,
            )
            tpk[...] += got[0:cap] + got[cap : 2 * cap] + got[2 * cap : 3 * cap]
        return 0

    lax.fori_loop(0, tiles // 2, finish, 0)

    ext[z] = scores[0:2, :]
    ext_copies = [
        pltpu.make_async_remote_copy(
            src_ref=ext.at[z], dst_ref=ext.at[z], send_sem=e_s.at[k],
            recv_sem=e_r.at[z], device_id=to, device_id_type=AT)
        for k, (_, to) in enumerate(stack)
    ]
    for copy in ext_copies:
        copy.start()

    top = jnp.max(scores[...], axis=1, keepdims=True)
    total = jnp.sum(jnp.exp(scores[...] - top), axis=1, keepdims=True)
    top_row, total_row = to_row(top, 128), to_row(total, 128)
    base = (z * cap).astype(F32)
    places_here = iota((cap, 128), 0).astype(F32) + base
    for t in range(groups):
        held = places_here == pp[t : t + 1, :]
        target = jnp.sum(
            jnp.where(held, tpk[:, t * 128 : (t + 1) * 128], 0.0), axis=0, keepdims=True
        )
        send_a[t] = jnp.concatenate([target, top_row, total_row], axis=1)
    recv_a[gx] = send_a[group]
    plane_copies = [
        pltpu.make_async_remote_copy(
            src_ref=send_a.at[p // 4], dst_ref=recv_a.at[gx], send_sem=a_s.at[k],
            recv_sem=a_r.at[gx], device_id=to, device_id_type=AT)
        for k, (p, to) in enumerate(peers)
    ]
    for copy in plane_copies:
        copy.start()

    for copy in sent:
        copy.wait_send()

    def ring_drain(jj, _):
        for way in range(2):
            for m in range(NZ - 1):
                for copy in ring_copies(m, jj * 2 + way, way):
                    copy.wait_send()
        return 0

    lax.fori_loop(0, tiles // 2, ring_drain, 0)
    for k, (p, to) in enumerate(reversed(peers)):
        landed(recv_a.at[p], a_r.at[p])
    parts = [recv_a[k] for k in range(PLANE)]
    tops = [p[:, 128:256] for p in parts]
    while len(tops) > 1:
        tops = [jnp.maximum(a, b) for a, b in zip(tops[::2], tops[1::2])]
    sums = [p[:, 256:384] * jnp.exp(p[:, 128:256] - tops[0]) for p in parts]
    wanted = [p[:, 0:128] for p in parts]
    while len(sums) > 1:
        sums = [a + b for a, b in zip(sums[::2], sums[1::2])]
        wanted = [a + b for a, b in zip(wanted[::2], wanted[1::2])]
    used = iota((1, 128), 1) < cap
    log_total = jnp.where(used, tops[0] + jnp.log(jnp.where(used, sums[0], 1.0)), 0.0)
    column = to_column(log_total, cap)
    here = places_here == pp[pl.ds(group, 1), :]
    mine_part = wanted[0] - jnp.sum(jnp.where(here, column, 0.0), axis=0, keepdims=True)
    send_b[...] = jnp.concatenate([mine_part, log_total], axis=1)
    recv_b[z] = send_b[...]
    b_copies = [
        pltpu.make_async_remote_copy(
            src_ref=send_b, dst_ref=recv_b.at[z], send_sem=b_s.at[k],
            recv_sem=b_r.at[z], device_id=to, device_id_type=AT)
        for k, (_, to) in enumerate(stack)
    ]
    for copy in b_copies:
        copy.start()
    for copy in plane_copies + ext_copies:
        copy.wait_send()
    for p, _ in stack:
        landed(ext.at[p], e_r.at[p])
    for p, _ in reversed(stack):
        landed(recv_b.at[p], b_r.at[p])

    margin = recv_b[0][:, 0:128]
    for k in range(1, NZ):
        margin = margin + recv_b[k][:, 0:128]
    margin = margin - vec[pl.ds(48 + group, 1), :]
    spare = vec[pl.ds(32 + group, 1), :] > 0.0
    climb = to_column(jnp.where(vec[pl.ds(40 + group, 1), :] > 0.0, BIG, margin), 128)
    least = jnp.min(jnp.where(reach[...] > 0.0, climb, BIG), axis=0, keepdims=True)
    both = jnp.where(
        iota((8, 128), 0) == 0,
        jnp.where(spare, 0.0, margin),
        jnp.where(spare, 0.0, least),
    )
    both = pltpu.roll(both, lax.rem(128 - 2 * HALF * lax.rem(gx, 4), 128), axis=1)
    out_v[...] = both[0:1, 0 : 2 * HALF]
    out_l[...] = both[1:2, 0 : 2 * HALF]
    lane = iota((1, 128), 1)
    for k in range(NZ):
        line = recv_b[k][:, 128:256]
        low = jnp.sum(jnp.where(lane == 0, line, 0.0), axis=1, keepdims=True)
        high = jnp.sum(jnp.where(lane == 1, line, 0.0), axis=1, keepdims=True)
        out_e[2 * k : 2 * k + 2, :] = ext[k] - jnp.where(iota((2, 1), 0) == 0, low, high)
    for copy in b_copies:
        copy.wait_send()


def fused(cap, number, vec, hidden, head):
    depth, width = head.shape
    nodes = hidden.shape[0] * PLANE
    rows, tiles, hops = cap * NZ, width // TILE, NZ - 1
    dma = pltpu.SemaphoreType.DMA
    vmem = pl.BlockSpec(memory_space=pltpu.VMEM)
    far = pl.BlockSpec(memory_space=pl.ANY)
    return pl.pallas_call(
        functools.partial(kernel, cap),
        out_shape=(
            jax.ShapeDtypeStruct((1, 2 * HALF), F32),
            jax.ShapeDtypeStruct((1, 2 * HALF), F32),
            jax.ShapeDtypeStruct((2 * NZ, width), F32),
        ),
        in_specs=[vmem, far, far],
        out_specs=(vmem, vmem, vmem),
        scratch_shapes=[
            pltpu.VMEM((depth, width), BF16),
            pltpu.VMEM((2, nodes, depth // 2), BF16),
            pltpu.VMEM((2, rows, depth // 2), BF16),
            pltpu.VMEM((rows, width), F32),
            pltpu.VMEM((rows, nodes), BF16),
            pltpu.VMEM((width, nodes), BF16),
            pltpu.VMEM((8, 128), F32),
            pltpu.VMEM((128, 128), F32),
            pltpu.VMEM((hops, tiles, cap, TILE), jnp.int16),
            pltpu.VMEM((hops, tiles, 1, TILE), F32),
            pltpu.VMEM((hops, tiles, cap, TILE), jnp.int16),
            pltpu.VMEM((hops, tiles, 1, TILE), F32),
            pltpu.VMEM((cap, width), F32),
            pltpu.VMEM((cap, nodes), F32),
            pltpu.VMEM((nodes // 128, 1, 384), F32),
            pltpu.VMEM((PLANE, 1, 384), F32),
            pltpu.VMEM((1, 256), F32),
            pltpu.VMEM((NZ, 1, 256), F32),
            pltpu.VMEM((NZ, 2, width), F32),
            dma((3,)),
            dma((2, 2, 31)),
            dma((2, 2, 4, 4)),
            dma((2, 2, 4, 4)),
            dma((hops, tiles)),
            dma((hops, tiles)),
            dma((hops, tiles)),
            dma((hops, tiles)),
            dma((PLANE,)),
            dma((PLANE,)),
            dma((NZ,)),
            dma((NZ,)),
            dma((NZ,)),
            dma((NZ,)),
        ],
        compiler_params=pltpu.CompilerParams(
            collective_id=number, has_side_effects=True, vmem_limit_bytes=67043328
        ),
        name=f"head_{cap}",
    )(vec, hidden, head)


def local(hidden, lm_head, parent, draft_token, draft_prob, uniforms, node_count, accepted_end):
    lines = (parent.shape[0] // 128, 128)
    vmem, smem = pl.BlockSpec(memory_space=pltpu.VMEM), pl.BlockSpec(memory_space=pltpu.SMEM)
    vec, which = pl.pallas_call(
        plan,
        out_shape=(
            jax.ShapeDtypeStruct((64, 128), F32),
            jax.ShapeDtypeStruct((1,), jnp.int32),
        ),
        in_specs=[vmem, smem, smem, vmem, vmem, vmem],
        out_specs=(vmem, smem),
        name="plan",
    )(
        parent.reshape(lines), node_count, accepted_end, draft_token.reshape(lines),
        draft_prob.reshape(lines), uniforms.reshape(lines),
    )
    branches = [functools.partial(fused, cap, i) for i, cap in enumerate(BLOCKS)]
    slack, least, extra = lax.switch(which[0], branches, vec, hidden, lm_head)
    return slack.reshape(-1), least.reshape(-1), extra


def solution(mesh):
    finer = Mesh(mesh.devices.reshape(NX, NY, NC, NZ), ALL)
    placed = (P(GX, "gy"), P("gy", GX), P(), P(), P(), P(), P(), P())
    return jax.shard_map(
        local, mesh=finer, in_specs=placed, out_specs=(P(GX), P(GX), P(None, GX)), check_vma=False
    )
```

time: 308 us -> 75.1 us (0.24)
  waiting for transfers between devices: 167 us -> 0 us
  local copies, waits for them, and re-layouts: 74.7 us -> 3.83 us
  Pallas kernels: 0 us -> 69.5 us
  other arithmetic: 15.4 us -> 0 us
  blocking collectives: 13.3 us -> 0 us
  between operations: 14.3 us -> 1.3 us
  starting transfers between devices: 11.8 us -> 0 us
  matrix products: 11 us -> 0 us
    reduce_scatter x1 -> x0, waiting for transfers between devices: 90.3 us -> none  [local(): lax.psum_scatter(jnp.dot(columns, lm_head, preferred_element_type=jnp.flo...]
    pallas_call x0 -> x2, Pallas kernels: none -> 69.5 us  [the longest x1 67.8 us: fused(): pl.pallas_call(functools.partial(kernel, cap), out_shape=(jax.ShapeDtypeS...]
    gather x16 -> x0, local copies, waits for them, and re-layouts: 64.9 us -> none  [the longest x6 27.2 us: local(): path_min = jnp.minimum(path_min, path_min[ancestor])]
    all_gather x2 -> x0, waiting for transfers between devices: 59 us -> none  [all_blocks(): tiles = lax.all_gather(tiles, axes[k], axis=0, tiled=True)]
    all_to_all x2 -> x0, waiting for transfers between devices: 17.8 us -> none  [from_everyone(): return lax.all_to_all(copies, axis, split_axis=0, concat_axis=0, tiled=True)]
    all_gather x1 -> x0, blocking collectives: 13.3 us -> none  [all_blocks(): tiles = lax.all_gather(tiles, axes[k], axis=0, tiled=True)]
    all_to_all x2 -> x0, starting transfers between devices: 11.7 us -> none  [from_everyone(): return lax.all_to_all(copies, axis, split_axis=0, concat_axis=0, tiled=True)]
    dot_general x1 -> x0, matrix products: 11 us -> none  [local(): jnp.dot(columns, lm_head, preferred_element_type=jnp.float32)]
  transfers between devices with their start and end apart: 5 -> 0, of which waited for: 5 -> 0; matrix products, arithmetic and copies ran while one was open for 9% -> 0% of each run, Pallas kernels for 0% -> 0%
where the time goes in v1:
time: 75.1 us; the launch traced here: 74.9 us
  Pallas kernels  69.5 us (93%)
  local copies, waits for them, and re-layouts  3.83 us (5%)
  between operations  1.3 us (2%)
    pallas_call x1, Pallas kernels, fused(): pl.pallas_call(functools.partial(kernel, cap), out_shape=(jax.ShapeDtypeS...  67.8 us
    unnamed x3, local copies, waits for them, and re-layouts  3.83 us
    pallas_call x1, Pallas kernels, local(): pl.pallas_call(plan, out_shape=(jax.ShapeDtypeStruct((64, 128), F32), jax...  1.78 us

profile of v1, /device:TPU:1, one launch (start us, length us, event | category | flops | bytes accessed | tf_op | source)
XLA Modules:
  0.0 74.9 jit_solution(8161569926809975874)
XLA Ops:
  0.6 1.8 %plan.1 = (f32[64,128]{1,0:T(8,128)}, s32[1]{0:T(128)}) custom-call(s32[8,128]{1,0:T(8,128)} %bitcast.11, s32[16]{0:T(128)} %counts.1, s32[16]{0:T(128)} %ends.1, s32[8,128]{1,0:T(8,128)} %bitcast.12, f32[8,128]{1,0:T(8,128)} %bitcast.13, f32[8,128]{1,0:T(8,128)} %bitcast.14), custom_call_target="tpu_custom_call" | custom-call | tf_op jit(solution)/shard_map/plan/pallas_call | solution.py:571
  3.1 68.0 %conditional.1 = (f32[16,2048]{1,0:T(8,128)}, f32[32]{0:T(128)}, f32[32]{0:T(128)}) conditional(s32[]{:T(128)} %bitcast.10, (f32[64,128]{1,0:T(8,128)}, bf16[32,2048]{1,0:T(8,128)(2,1)}, bf16[2048,2048]{1,0:T(8,128)(2,1)}) %tuple.26, (f32[64,128]{1,0:T(8,128)}, bf16[32,2048]{1,0:T(8,128)(2,1)}, ...), branch_computations={%region_0.0_spmd, %region_1.0_spmd, %region_2.0_spmd} | conditional | bytes 24 | solution.py:585
  3.1 67.8 %head_48.1 = (f32[1,32]{1,0:T(1,128)}, f32[1,32]{1,0:T(1,128)}, f32[16,2048]{1,0:T(8,128)}) custom-call(f32[64,128]{1,0:T(8,128)} %get-tuple-element.29.vec, bf16[32,2048]{1,0:T(8,128)(2,1)} %get-tuple-element.30.own, bf16[2048,2048]{1,0:T(8,128)(2,1)} %get-tuple-element.31.head), custom_call_target="tpu_custom_call" | custom-call | tf_op jit(solution)/shard_map/cond/branch_0_fun/head_48/pallas_call | solution.py:517
  71.1 1.1 %copy.23 = f32[32]{0:T(128)} copy(f32[32]{0:T(128)} %get-tuple-element.72) | data formatting | bytes 256
  72.2 1.1 %copy.24 = f32[32]{0:T(128)} copy(f32[32]{0:T(128)} %get-tuple-element.73) | data formatting | bytes 256
  73.3 1.6 %copy.25 = f32[16,2048]{1,0:T(8,128)} copy(f32[16,2048]{1,0:T(8,128)} %get-tuple-element.74) | data formatting | bytes 262144
